TPU v7x, 32 devices: a whole 2x2x4 slice. The times are simulated.
32 devices in a mesh: dp: 16 (over z, x, core), tensor: 2 (over y).
Axes of the slice: x: 2, y: 2, z: 4, core: 2. Of those that a mesh axis runs over, the one named last changes fastest.
Arguments:
- tokens: bfloat16 [16, 736, 1152], P('dp', 'tensor'), may hold values from -6 to 6
- cotangent: bfloat16 [16, 736, 1152], P('dp', 'tensor'), may hold values from -6 to 6
- counts: int32 [16], P('dp'), may hold values from 638 to 729
- joint_weight: float32 [1152, 3, 1152], P('dp', None, 'tensor'), may hold values from -0.1875 to 0.1875
- joint_moment: float32 [1152, 3, 1152], P('dp', None, 'tensor'), may hold values from -0.0014648438 to 0.0014648438
- joint_square: float32 [1152, 3, 1152], P('dp', None, 'tensor'), may hold values from 4.53793e-09 to 3.630344e-08
- output_weight: float32 [1152, 1152], P('tensor', 'dp'), may hold values from -0.5 to 0.5
- output_moment: float32 [1152, 1152], P('tensor', 'dp'), may hold values from -0.0029296875 to 0.0029296875
- output_square: float32 [1152, 1152], P('tensor', 'dp'), may hold values from 1.815172e-08 to 1.4521376e-07
- expand_weight: float32 [1152, 4304], P('dp', 'tensor'), may hold values from -0.1875 to 0.1875
- expand_moment: float32 [1152, 4304], P('dp', 'tensor'), may hold values from -0.0029296875 to 0.0029296875
- expand_square: float32 [1152, 4304], P('dp', 'tensor'), may hold values from 1.815172e-08 to 1.4521376e-07
- reduce_weight: float32 [4304, 1152], P('tensor', 'dp'), may hold values from -0.09375 to 0.09375
- reduce_moment: float32 [4304, 1152], P('tensor', 'dp'), may hold values from -0.005859375 to 0.005859375
- reduce_square: float32 [4304, 1152], P('tensor', 'dp'), may hold values from 7.260688e-08 to 5.8085504e-07
- norm_gains: float32 [2, 1152], replicated, may hold values from 0.5 to 1.5
- gains_moment: float32 [2, 1152], replicated, may hold values from -0.009765625 to 0.009765625
- gains_square: float32 [2, 1152], replicated, may hold values from 2.0168576e-07 to 1.6134861e-06
- shifts: float32 [4, 1152], replicated, may hold values from -3 to 3
- shifts_moment: float32 [4, 1152], replicated, may hold values from -0.009765625 to 0.009765625
- shifts_square: float32 [4, 1152], replicated, may hold values from 2.0168576e-07 to 1.6134861e-06
- head_bias: float32 [2, 1152], P(None, 'tensor'), may hold values from -3 to 3
- head_moment: float32 [2, 1152], P(None, 'tensor'), may hold values from -0.0029296875 to 0.0029296875
- head_square: float32 [2, 1152], P(None, 'tensor'), may hold values from 1.815172e-08 to 1.4521376e-07
- hidden_bias: float32 [4304], P('tensor'), may hold values from -3 to 3
- hidden_moment: float32 [4304], P('tensor'), may hold values from -0.0029296875 to 0.0029296875
- hidden_square: float32 [4304], P('tensor'), may hold values from 1.815172e-08 to 1.4521376e-07
Outputs:
- layer_out: bfloat16 [16, 736, 1152], P('dp', 'tensor')
- input_grad: bfloat16 [16, 736, 1152], P('dp', 'tensor')
- grad_norm: float32 [], replicated
- joint_new: float32 [1152, 3, 1152], P('dp', None, 'tensor')
- joint_moment_new: float32 [1152, 3, 1152], P('dp', None, 'tensor')
- joint_square_new: float32 [1152, 3, 1152], P('dp', None, 'tensor')
- joint_copy: bfloat16 [1152, 3, 1152], P('dp', None, 'tensor')
- output_new: float32 [1152, 1152], P('tensor', 'dp')
- output_moment_new: float32 [1152, 1152], P('tensor', 'dp')
- output_square_new: float32 [1152, 1152], P('tensor', 'dp')
- output_copy: bfloat16 [1152, 1152], P('tensor', 'dp')
- expand_new: float32 [1152, 4304], P('dp', 'tensor')
- expand_moment_new: float32 [1152, 4304], P('dp', 'tensor')
- expand_square_new: float32 [1152, 4304], P('dp', 'tensor')
- expand_copy: bfloat16 [1152, 4304], P('dp', 'tensor')
- reduce_new: float32 [4304, 1152], P('tensor', 'dp')
- reduce_moment_new: float32 [4304, 1152], P('tensor', 'dp')
- reduce_square_new: float32 [4304, 1152], P('tensor', 'dp')
- reduce_copy: bfloat16 [4304, 1152], P('tensor', 'dp')
- gains_new: float32 [2, 1152], replicated
- gains_moment_new: float32 [2, 1152], replicated
- gains_square_new: float32 [2, 1152], replicated
- shifts_new: float32 [4, 1152], replicated
- shifts_moment_new: float32 [4, 1152], replicated
- shifts_square_new: float32 [4, 1152], replicated
- head_new: float32 [2, 1152], P(None, 'tensor')
- head_moment_new: float32 [2, 1152], P(None, 'tensor')
- head_square_new: float32 [2, 1152], P(None, 'tensor')
- hidden_new: float32 [4304], P('tensor')
- hidden_moment_new: float32 [4304], P('tensor')
- hidden_square_new: float32 [4304], P('tensor')
Inputs may be any that keep to these rules, and one draw needn't show every extreme that they name: `counts`: valid tokens of each image; key slots from there up to 736 are padding.
All inputs are finite; a program needn't handle non-finite values.
Results may differ from a plain program's by a relative error of at most 0.01.
Values may be sent and summed in bfloat16 or wider, within the bound.
A program may use at most 192 MiB of HBM per device.

v0:
```python
import jax
import jax.numpy as jnp
from jax import lax
from jax.sharding import PartitionSpec as P

HD = 72
STEP = 4
norm_eps = 1e-06
clip_limit = 1.0
matrix_rate = 0.03
vector_rate = 0.3
decay_rate = 0.1
adam_eps = 1e-08
mask_fill = -1e30


def layer_norm(values, gain, shift):
    center = jnp.mean(values, axis=-1, keepdims=True)
    centred = values - center
    spread = jnp.mean(centred * centred, axis=-1, keepdims=True)
    return centred * lax.rsqrt(spread + norm_eps) * gain + shift


def gelu_tanh(values):
    return jax.nn.gelu(values, approximate=True)


def whole_rows(part):
    return lax.all_gather(part, "tensor", axis=1, tiled=True)


def share_rows(full):
    return lax.psum_scatter(
        full.astype(jnp.bfloat16), "tensor", scatter_dimension=1, tiled=True
    ).astype(jnp.float32)


def scatter_sum(part, dim):
    return lax.psum_scatter(
        part.astype(jnp.bfloat16), "dp", scatter_dimension=dim, tiled=True
    ).astype(jnp.float32)


def split_heads(joint):
    length = joint.shape[0]
    heads_local = joint.shape[2] // HD
    query = joint[:, 0].reshape(length, heads_local, HD)
    keys = joint[:, 1].reshape(length, heads_local, HD)
    values = joint[:, 2].reshape(length, heads_local, HD)
    return (query, keys, values)


def masked_scores(query, keys, count):
    length = query.shape[0]
    scores = jnp.einsum("qhd,khd->hqk", query, keys, preferred_element_type=jnp.float32) * HD ** (
        -0.5
    )
    valid = jnp.arange(length, dtype=jnp.int32) < count
    return jnp.where(valid[None, None, :], scores, mask_fill)


def attend(joint, count):
    query, keys, values = split_heads(joint)
    scores = masked_scores(query, keys, count)
    top = jnp.max(scores, axis=-1, keepdims=True)
    total = jnp.sum(jnp.exp(scores - top), axis=-1, keepdims=True)
    logsum = top + jnp.log(total)
    probs = jnp.exp(scores - logsum)
    mixed = jnp.einsum(
        "hqk,khd->qhd", probs.astype(jnp.bfloat16), values, preferred_element_type=jnp.float32
    )
    return (mixed.reshape(joint.shape[0], joint.shape[2]).astype(jnp.bfloat16), logsum[:, :, 0])


def attend_back(joint, mixed_grad, logsum, count):
    query, keys, values = split_heads(joint)
    length = joint.shape[0]
    grad_heads = mixed_grad.reshape(length, joint.shape[2] // HD, HD)
    scores = masked_scores(query, keys, count)
    probs = jnp.exp(scores - logsum[:, :, None])
    value_grad = jnp.einsum(
        "hqk,qhd->khd", probs.astype(jnp.bfloat16), grad_heads, preferred_element_type=jnp.float32
    )
    prob_grad = jnp.einsum("qhd,khd->hqk", grad_heads, values, preferred_element_type=jnp.float32)
    inner = jnp.sum(probs * prob_grad, axis=-1, keepdims=True)
    score_grad = (probs * (prob_grad - inner)).astype(jnp.bfloat16)
    query_grad = jnp.einsum(
        "hqk,khd->qhd", score_grad, keys, preferred_element_type=jnp.float32
    ) * HD ** (-0.5)
    key_grad = jnp.einsum(
        "hqk,qhd->khd", score_grad, query, preferred_element_type=jnp.float32
    ) * HD ** (-0.5)
    stacked = jnp.stack([query_grad, key_grad, value_grad], axis=1)
    return stacked.reshape(length, 3, joint.shape[2]).astype(jnp.bfloat16)


def forward_pass(tokens, counts, weights, small):
    joint_w, expand_w, output_w, reduce_w = weights
    norm_gains, shifts, head_bias, hidden_bias = small
    rows = tokens.astype(jnp.float32)
    normed, first_back = jax.vjp(layer_norm, rows, norm_gains[0], shifts[0])
    normed_whole = whole_rows(normed.astype(jnp.bfloat16))
    joint = jnp.einsum("bsd,dch->bsch", normed_whole, joint_w, preferred_element_type=jnp.float32)
    bias = jnp.stack([head_bias[0], jnp.zeros_like(head_bias[0]), head_bias[1]])
    joint = (joint + bias).astype(jnp.bfloat16)
    mixed, logsum = lax.map(lambda pair: attend(pair[0], pair[1]), (joint, counts))
    branch = (
        share_rows(jnp.einsum("bsh,hd->bsd", mixed, output_w, preferred_element_type=jnp.float32))
        + shifts[2]
    )
    middle = rows + branch
    second, second_back = jax.vjp(layer_norm, middle, norm_gains[1], shifts[1])
    second_whole = whole_rows(second.astype(jnp.bfloat16))
    before = (
        jnp.einsum("bsd,df->bsf", second_whole, expand_w, preferred_element_type=jnp.float32)
        + hidden_bias
    )
    active, gelu_back = jax.vjp(gelu_tanh, before)
    active = active.astype(jnp.bfloat16)
    result = (
        share_rows(jnp.einsum("bsf,fd->bsd", active, reduce_w, preferred_element_type=jnp.float32))
        + shifts[3]
    )
    saved = (
        first_back,
        normed_whole,
        joint,
        mixed,
        logsum,
        second_back,
        second_whole,
        active,
        gelu_back,
    )
    return (middle + result, saved)


def adamw_step(weight, grad, moment, square, factor, rate, decay):
    clipped = grad * factor
    moment_new = 0.5 * moment + 0.5 * clipped
    square_new = 0.5 * square + 0.5 * clipped * clipped
    correct = 1.0 - 0.5**STEP
    update = moment_new / correct / (jnp.sqrt(square_new / correct) + adam_eps)
    return (weight - rate * (update + decay * weight), moment_new, square_new)


def squares(values):
    return jnp.sum(values * values)


def on_device(
    tokens,
    cotangent,
    counts,
    joint_weight,
    joint_moment,
    joint_square,
    output_weight,
    output_moment,
    output_square,
    expand_weight,
    expand_moment,
    expand_square,
    reduce_weight,
    reduce_moment,
    reduce_square,
    norm_gains,
    gains_moment,
    gains_square,
    shifts,
    shifts_moment,
    shifts_square,
    head_bias,
    head_moment,
    head_square,
    hidden_bias,
    hidden_moment,
    hidden_square,
):
    first_pair = (
        lax.all_gather(joint_weight.astype(jnp.bfloat16), "dp", axis=0, tiled=True),
        lax.all_gather(expand_weight.astype(jnp.bfloat16), "dp", axis=0, tiled=True),
    )
    second_pair = (
        lax.all_gather(output_weight.astype(jnp.bfloat16), "dp", axis=1, tiled=True),
        lax.all_gather(reduce_weight.astype(jnp.bfloat16), "dp", axis=1, tiled=True),
    )
    weights = (first_pair[0], first_pair[1], second_pair[0], second_pair[1])
    small = (norm_gains, shifts, head_bias, hidden_bias)
    layer_rows, saved = forward_pass(tokens, counts, weights, small)
    layer_out = layer_rows.astype(jnp.bfloat16)
    first_back, normed_whole, joint, mixed, logsum, second_back, second_whole, active, gelu_back = (
        saved
    )
    joint_w, expand_w, output_w, reduce_w = weights
    grad_rows = cotangent.astype(jnp.float32)
    grad_whole = whole_rows(cotangent)
    reduce_grad = jnp.einsum("bsf,bsd->fd", active, grad_whole, preferred_element_type=jnp.float32)
    active_grad = jnp.einsum(
        "bsd,fd->bsf", grad_whole, reduce_w, preferred_element_type=jnp.float32
    )
    before_grad = gelu_back(active_grad)[0].astype(jnp.bfloat16)
    expand_grad = jnp.einsum(
        "bsd,bsf->df", second_whole, before_grad, preferred_element_type=jnp.float32
    )
    hidden_grad = jnp.sum(before_grad, axis=(0, 1), dtype=jnp.float32)
    second_grad = share_rows(
        jnp.einsum("bsf,df->bsd", before_grad, expand_w, preferred_element_type=jnp.float32)
    )
    middle_part, gain_two, shift_two = second_back(second_grad)
    middle_grad = grad_rows + middle_part
    branch_grad = middle_grad.astype(jnp.bfloat16)
    branch_whole = whole_rows(branch_grad)
    output_grad = jnp.einsum("bsh,bsd->hd", mixed, branch_whole, preferred_element_type=jnp.float32)
    mixed_grad = jnp.einsum(
        "bsd,hd->bsh", branch_whole, output_w, preferred_element_type=jnp.float32
    ).astype(jnp.bfloat16)
    joint_grad = lax.map(
        lambda group: attend_back(group[0], group[1], group[2], group[3]),
        (joint, mixed_grad, logsum, counts),
    )
    joint_weight_grad = jnp.einsum(
        "bsd,bsch->dch", normed_whole, joint_grad, preferred_element_type=jnp.float32
    )
    head_grad = jnp.sum(joint_grad[:, :, 0::2], axis=(0, 1), dtype=jnp.float32)
    first_grad = share_rows(
        jnp.einsum("bsch,dch->bsd", joint_grad, joint_w, preferred_element_type=jnp.float32)
    )
    rows_part, gain_one, shift_one = first_back(first_grad)
    input_grad = (middle_grad + rows_part).astype(jnp.bfloat16)
    gain_grad = jnp.stack([gain_one, gain_two])
    shift_grad = jnp.stack(
        [
            shift_one,
            shift_two,
            jnp.sum(branch_grad, axis=(0, 1), dtype=jnp.float32),
            jnp.sum(grad_rows, axis=(0, 1)),
        ]
    )
    joint_sum, expand_sum = (scatter_sum(joint_weight_grad, 0), scatter_sum(expand_grad, 0))
    output_sum, reduce_sum = (scatter_sum(output_grad, 1), scatter_sum(reduce_grad, 1))
    gain_sum, shift_sum = lax.psum((gain_grad, shift_grad), ("dp", "tensor"))
    head_sum, hidden_sum = lax.psum((head_grad, hidden_grad), "dp")
    data_count = lax.axis_size("dp")
    split_count = lax.axis_size("tensor")
    owned = squares(joint_sum) + squares(expand_sum) + squares(output_sum) + squares(reduce_sum)
    shared = (squares(head_sum) + squares(hidden_sum)) / data_count
    everywhere = (squares(gain_sum) + squares(shift_sum)) / (data_count * split_count)
    grad_norm = jnp.sqrt(lax.psum(owned + shared + everywhere, ("dp", "tensor")))
    factor = clip_limit / jnp.maximum(grad_norm, clip_limit)
    joint_state = adamw_step(
        joint_weight, joint_sum, joint_moment, joint_square, factor, matrix_rate, decay_rate
    )
    output_state = adamw_step(
        output_weight, output_sum, output_moment, output_square, factor, matrix_rate, decay_rate
    )
    expand_state = adamw_step(
        expand_weight, expand_sum, expand_moment, expand_square, factor, matrix_rate, decay_rate
    )
    reduce_state = adamw_step(
        reduce_weight, reduce_sum, reduce_moment, reduce_square, factor, matrix_rate, decay_rate
    )
    gains_state = adamw_step(
        norm_gains, gain_sum, gains_moment, gains_square, factor, vector_rate, 0.0
    )
    shifts_state = adamw_step(
        shifts, shift_sum, shifts_moment, shifts_square, factor, vector_rate, 0.0
    )
    head_state = adamw_step(head_bias, head_sum, head_moment, head_square, factor, vector_rate, 0.0)
    hidden_state = adamw_step(
        hidden_bias, hidden_sum, hidden_moment, hidden_square, factor, vector_rate, 0.0
    )
    return (
        layer_out,
        input_grad,
        grad_norm,
        joint_state[0],
        joint_state[1],
        joint_state[2],
        joint_state[0].astype(jnp.bfloat16),
        output_state[0],
        output_state[1],
        output_state[2],
        output_state[0].astype(jnp.bfloat16),
        expand_state[0],
        expand_state[1],
        expand_state[2],
        expand_state[0].astype(jnp.bfloat16),
        reduce_state[0],
        reduce_state[1],
        reduce_state[2],
        reduce_state[0].astype(jnp.bfloat16),
        gains_state[0],
        gains_state[1],
        gains_state[2],
        shifts_state[0],
        shifts_state[1],
        shifts_state[2],
        head_state[0],
        head_state[1],
        head_state[2],
        hidden_state[0],
        hidden_state[1],
        hidden_state[2],
    )


def solution(mesh):
    in_specs = (
        P("dp", "tensor", None),
        P("dp", "tensor", None),
        P("dp"),
        P("dp", None, "tensor"),
        P("dp", None, "tensor"),
        P("dp", None, "tensor"),
        P("tensor", "dp"),
        P("tensor", "dp"),
        P("tensor", "dp"),
        P("dp", "tensor"),
        P("dp", "tensor"),
        P("dp", "tensor"),
        P("tensor", "dp"),
        P("tensor", "dp"),
        P("tensor", "dp"),
        P(),
        P(),
        P(),
        P(),
        P(),
        P(),
        P(None, "tensor"),
        P(None, "tensor"),
        P(None, "tensor"),
        P("tensor"),
        P("tensor"),
        P("tensor"),
    )
    out_specs = (
        P("dp", "tensor", None),
        P("dp", "tensor", None),
        P(),
        P("dp", None, "tensor"),
        P("dp", None, "tensor"),
        P("dp", None, "tensor"),
        P("dp", None, "tensor"),
        P("tensor", "dp"),
        P("tensor", "dp"),
        P("tensor", "dp"),
        P("tensor", "dp"),
        P("dp", "tensor"),
        P("dp", "tensor"),
        P("dp", "tensor"),
        P("dp", "tensor"),
        P("tensor", "dp"),
        P("tensor", "dp"),
        P("tensor", "dp"),
        P("tensor", "dp"),
        P(),
        P(),
        P(),
        P(),
        P(),
        P(),
        P(None, "tensor"),
        P(None, "tensor"),
        P(None, "tensor"),
        P("tensor"),
        P("tensor"),
        P("tensor"),
    )
    return jax.shard_map(
        on_device, mesh=mesh, in_specs=in_specs, out_specs=out_specs, check_vma=False
    )
```

profile of v0, /device:TPU:0, one launch (start us, length us, event | category | flops | bytes accessed | tf_op | source)
XLA Modules:
  0.0 853.5 jit_solution(2574007469518018370)
XLA Ops:
  17.5 29.0 %all-gather.9.cloned.1.call-done = bf16[1,736,1152]{2,1,0:T(8,128)(2,1)} async-done(((bf16[1,368,1152]{2,1,0:T(8,128)(2,1)}), bf16[1,736,1152]{2,1,0:T(8,128)(2,1)}) %all-gather.9.cloned.1.call-update) | async-done | bytes 1695760 | tf_op jit(solution)/shard_map/all_gather | solution.py:29
  46.5 54.5 %all-gather.11.cloned.1.call-done = bf16[1152,3,576]{2,0,1:T(8,128)(2,1)} async-done(((bf16[72,3,576]{2,0,1:T(8,128)(2,1)}), bf16[1152,3,576]{2,0,1:T(8,128)(2,1)}) %all-gather.11.cloned.1.call-update) | async-done | bytes 3981328 | tf_op jit(solution)/shard_map/all_gather | solution.py:181
  101.0 6.4 add_convert_fusion
  107.7 8.6 %fusion = (f32[8,736]{1,0:T(8,128)S(1)}, f32[8,736,736]{1,2,0:T(8,128)}) fusion(pred[736]{0:T(1024)(128)(4,1)S(1)} %iota_compare_fusion, bf16[736,8,72]{0,2,1:T(8,128)(2,1)S(1)} %bitcast.96, bf16[736,8,72]{0,2,1:T(8,128)(2,1)S(1)} %bitcast.94), kind=kOutput, calls=%fused_computation.5 | convolution fusion | flops 637028608 | bytes 19054304 | tf_op jit(solution)/shard_map/while/body/eval_jaxpr/qhd,khd->hqk/dot_general | solution.py:55
  116.3 10.0 %exponential_reduce_fusion = f32[8,736]{1,0:T(8,128)S(1)} fusion(f32[8,736,736]{1,2,0:T(8,128)} %get-tuple-element.122, f32[8,736]{1,0:T(8,128)S(1)} %get-tuple-element.121, pred[736]{0:T(1024)(128)(4,1)S(1)} %iota_compare_fusion), kind=kLoop, calls=%fused_computation.3 | loop fusion | flops 17328384 | bytes 17382112 | tf_op jit(solution)/shard_map/while/body/eval_jaxpr/reduce_sum | solution.py:66
  126.3 8.2 fusion.1
  146.9 25.5 %reduce-scatter.17.cloned.1.call-done = bf16[1,368,1152]{2,1,0:T(8,128)(2,1)} async-done(((bf16[1,736,1152]{2,1,0:T(8,128)(2,1)}), bf16[1,368,1152]{2,1,0:T(8,128)(2,1)}) %reduce-scatter.17.cloned.1.call-update) | async-done | bytes 847888 | tf_op jit(solution)/shard_map/reduce_scatter | solution.py:33
  179.3 50.8 %all-gather.17.cloned.1.call-done = bf16[1152,2152]{1,0:T(8,128)(2,1)} async-done(((bf16[72,2152]{1,0:T(8,128)(2,1)}), bf16[1152,2152]{1,0:T(8,128)(2,1)}) %all-gather.17.cloned.1.call-update) | async-done | bytes 4958224 | tf_op jit(solution)/shard_map/all_gather | solution.py:182
  230.1 29.2 %all-gather.15.cloned.1.call-done = bf16[1,736,1152]{2,1,0:T(8,128)(2,1)} async-done(((bf16[1,368,1152]{2,1,0:T(8,128)(2,1)}), bf16[1,736,1152]{2,1,0:T(8,128)(2,1)}) %all-gather.15.cloned.1.call-update) | async-done | bytes 1695760 | tf_op jit(solution)/shard_map/all_gather | solution.py:29
  259.4 10.1 %fusion.38 = f32[736,2152]{1,0:T(8,128)} fusion(bf16[1152,2152]{1,0:T(8,128)(2,1)} %all-gather.17.cloned.1.call-done, bf16[1,736,1152]{2,1,0:T(8,128)(2,1)} %all-gather.15.cloned.1.call-done), kind=kOutput, calls=%fused_computation.72 | convolution fusion | flops 3649241088 | bytes 12989440 | tf_op jit(solution)/shard_map/bsd,df->bsf/dot_general | solution.py:115
  269.5 20.1 %all-gather.21.cloned.1.call-done = bf16[1,736,1152]{2,1,0:T(8,128)(2,1)} async-done(((bf16[1,368,1152]{2,1,0:T(8,128)(2,1)}), bf16[1,736,1152]{2,1,0:T(8,128)(2,1)}) %all-gather.21.cloned.1.call-update) | async-done | bytes 1695760 | tf_op jit(solution)/shard_map/all_gather | solution.py:29
  289.6 57.9 %all-gather.19.cloned.1.call-done = bf16[2152,1152]{0,1:T(8,128)(2,1)} async-done(((bf16[2152,72]{0,1:T(8,128)(2,1)}), bf16[2152,1152]{0,1:T(8,128)(2,1)}) %all-gather.19.cloned.1.call-update) | async-done | bytes 4958224 | tf_op jit(solution)/shard_map/all_gather | solution.py:186
  347.5 11.3 %convert_reduce_fusion = (f32[2152]{0:T(1024)S(1)}, bf16[736,2152]{1,0:T(8,128)(2,1)S(1)}) fusion(f32[736,2152]{1,0:T(8,128)} %fusion.38, f32[2152]{0:T(1024)S(1)} %copy-done.46, bf16[2152,1152]{0,1:T(8,128)(2,1)} %all-gather.19.cloned.1.call-done, bf16[1,736,1152]{2,1,0:T(8,128)(2,1)} %all-gather.21.cloned.1.call-done), kind=kOutput, calls=%fused_computation.18 | convolution fusion | flops 3685668096 | bytes 16174400 | tf_op jit(solution)/shard_map/bsd,fd->bsf/dot_general | solution.py:199
  360.5 8.2 fusion.13
  368.9 11.1 %fusion.12 = bf16[1,736,1152]{2,1,0:T(8,128)(2,1)} fusion(bf16[2152,1152]{0,1:T(8,128)(2,1)} %all-gather.19.cloned.1.call-done, f32[736,2152]{1,0:T(8,128)} %fusion.38, f32[2152]{0:T(1024)S(1)} %copy-done.46), kind=kOutput, calls=%fused_computation.31 | convolution fusion | flops 3665927680 | bytes 12998048 | tf_op jit(solution)/shard_map/bsf,fd->bsd/dot_general | solution.py:121
  380.1 14.7 %reduce-scatter.21.cloned.1.call-done = bf16[1,368,1152]{2,1,0:T(8,128)(2,1)} async-done(((bf16[1,736,1152]{2,1,0:T(8,128)(2,1)}), bf16[1,368,1152]{2,1,0:T(8,128)(2,1)}) %reduce-scatter.21.cloned.1.call-update) | async-done | bytes 847888 | tf_op jit(solution)/shard_map/reduce_scatter | solution.py:33
  396.8 27.5 %reduce-scatter.19.cloned.1.call-done = bf16[1,368,1152]{2,1,0:T(8,128)(2,1)} async-done(((bf16[1,736,1152]{2,1,0:T(8,128)(2,1)}), bf16[1,368,1152]{2,1,0:T(8,128)(2,1)}) %reduce-scatter.19.cloned.1.call-update) | async-done | bytes 847888 | tf_op jit(solution)/shard_map/reduce_scatter | solution.py:33
  429.0 28.7 %all-gather.23.cloned.1.call-done = bf16[1,736,1152]{2,1,0:T(8,128)(2,1)} async-done(((bf16[1,368,1152]{2,1,0:T(8,128)(2,1)}), bf16[1,736,1152]{2,1,0:T(8,128)(2,1)}) %all-gather.23.cloned.1.call-update) | async-done | bytes 1695760 | tf_op jit(solution)/shard_map/all_gather | solution.py:29
  462.4 10.1 %convolution_convert_fusion = bf16[2152,1152]{0,1:T(8,128)(2,1)} fusion(bf16[1,736,1152]{2,1,0:T(8,128)(2,1)} %all-gather.21.cloned.1.call-done, f32[736,2152]{1,0:T(8,128)} %fusion.38, f32[2152]{0:T(1024)S(1)} %copy-done.46), kind=kOutput, calls=%fused_computation.6 | convolution fusion | flops 3667558912 | bytes 12998048 | tf_op jit(solution)/shard_map/bsf,bsd->fd/dot_general | solution.py:198
  472.6 9.1 %convolution_convert_fusion.1 = bf16[1152,2152]{1,0:T(8,128)(2,1)} fusion(bf16[736,2152]{1,0:T(8,128)(2,1)} %copy-done.47, bf16[1,736,1152]{2,1,0:T(8,128)(2,1)} %all-gather.15.cloned.1.call-done), kind=kOutput, calls=%fused_computation.7 | convolution fusion | flops 3651720192 | bytes 9821696 | tf_op jit(solution)/shard_map/bsd,bsf->df/dot_general | solution.py:203
  485.0 6.4 convolution_convert_fusion.7
  491.4 13.2 %multiply_reduce_fusion = (f32[8,736]{1,0:T(8,128)S(1)}, f32[8,736,736]{1,2,0:T(8,128)}) fusion(f32[8,736,736]{1,2,0:T(8,128)} %get-tuple-element.122, f32[8,736]{1,0:T(8,128)S(1)} %log_add_fusion, pred[736]{0:T(1024)(128)(4,1)S(1)} %iota_compare_fusion, bf16[736,8,72]{0,2,1:T(8,128)(2,1)S(1)} %bitcast.108, bf16[736,8,72]{0,2,1:T(8,128)(2,1)S(1)} %bitcast.93), kind=kOutput, calls=%fused_computation.1 | convolution fusion | flops 645695744 | bytes 36412128 | tf_op jit(solution)/shard_map/while/body/eval_jaxpr/qhd,khd->hqk/dot_general | solution.py:84
  504.6 13.0 %multiply_convert_fusion = bf16[8,736,736]{1,2,0:T(8,128)(2,1)S(1)} fusion(f32[8,736,736]{1,2,0:T(8,128)} %get-tuple-element.124, f32[8,736,736]{1,2,0:T(8,128)} %get-tuple-element.122, f32[8,736]{1,0:T(8,128)S(1)} %get-tuple-element.123, f32[8,736]{1,0:T(8,128)S(1)} %log_add_fusion, pred[736]{0:T(1024)(128)(4,1)S(1)} %iota_compare_fusion), kind=kLoop, calls=%fused_computation | loop fusion | flops 26001408 | bytes 43383520 | tf_op jit(solution)/shard_map/while/body/eval_jaxpr/convert_element_type | solution.py:86
  528.8 6.3 convolution_convert_fusion.2
  535.2 18.2 %copy.70 = bf16[1152,3,576]{2,1,0:T(4,128)(2,1)} copy(bf16[1152,3,576]{2,0,1:T(8,128)(2,1)S(1)} %convolution_convert_fusion.2) | data formatting | bytes 7962624
  553.4 12.4 %reshape.392 = bf16[1152,1728]{1,0:T(8,128)(2,1)} reshape(bf16[1152,3,576]{2,1,0:T(4,128)(2,1)} %copy.70) | data formatting | bytes 7962624
  568.3 62.1 %all-reduce.4 = (f32[2,576]{1,0:T(2,128)S(1)}, f32[2152]{0:T(1024)S(1)}) all-reduce(f32[2,576]{1,0:T(2,128)S(1)} %convert_reduce_fusion.1, f32[2152]{0:T(1024)S(1)} %get-tuple-element.125), channel_id=1, replica_groups=mesh['dp'=16,'tensor'=2] {'dp'}, use_global_device_ids=true, to_apply=%region_24.25 | all-reduce | flops 3304 | bytes 26432 | tf_op jit(solution)/shard_map/psum | solution.py:243
  636.3 47.3 %reduce-scatter.27.cloned.1.call-done = bf16[72,2152]{1,0:T(8,128)(2,1)} async-done(((bf16[1152,2152]{1,0:T(8,128)(2,1)}), bf16[72,2152]{1,0:T(8,128)(2,1)}) %reduce-scatter.27.cloned.1.call-update) | async-done | bytes 309904
  685.4 26.8 %reduce-scatter.23.cloned.1.call-done = bf16[1,368,1152]{2,1,0:T(8,128)(2,1)} async-done(((bf16[1,736,1152]{2,1,0:T(8,128)(2,1)}), bf16[1,368,1152]{2,1,0:T(8,128)(2,1)}) %reduce-scatter.23.cloned.1.call-update) | async-done | bytes 847888 | tf_op jit(solution)/shard_map/reduce_scatter | solution.py:33
  717.9 40.8 %all-reduce.3 = (f32[2,1152]{1,0:T(2,128)S(1)}, f32[4,1152]{1,0:T(4,128)S(1)}) all-reduce(f32[2,1152]{1,0:T(2,128)S(1)} %pad_maximum_fusion.6, f32[4,1152]{1,0:T(4,128)S(1)} %pad_maximum_fusion.4), channel_id=1, replica_groups=mesh['dp'=16,'tensor'=2] {'dp','tensor'}, use_global_device_ids=true, to_apply=%region_31.32 | all-reduce | flops 6912 | bytes 55296 | tf_op jit(solution)/shard_map/psum | solution.py:242
  761.3 27.2 %reduce-scatter.25.cloned.1.call-done = bf16[72,1728]{1,0:T(8,128)(2,1)} async-done(((bf16[1152,1728]{1,0:T(8,128)(2,1)}), bf16[72,1728]{1,0:T(8,128)(2,1)}) %reduce-scatter.25.cloned.1.call-update) | async-done | bytes 248848
  793.0 39.4 %psum.39 = f32[]{:T(128)} all-reduce(f32[]{:T(128)S(6)} %add.313), channel_id=1, replica_groups=mesh['dp'=16,'tensor'=2] {'dp','tensor'}, use_global_device_ids=true, to_apply=%region_39.40 | all-reduce | flops 1 | bytes 8 | tf_op jit(solution)/shard_map/psum | solution.py:249
  (202 shorter events, 86.5 us)
Async XLA Ops:
  7.2 39.3 %all-gather.9.cloned.1.call-start = ((), (), s32[]{:S(2)}) async-start(), calls=%async_computation.8 | async-start | bytes 2543616 | tf_op jit(solution)/shard_map/all_gather | solution.py:29
  8.7 98.8 %copy-start.35 = (f32[368]{0:T(512)}, f32[368]{0:T(512)S(1)}, u32[]{:S(2)}) copy-start(f32[368]{0:T(512)S(1)} %broadcast_multiply_fusion.1) | copy-start | bytes 4420
  10.8 96.6 %copy-start.38 = (f32[368]{0:T(512)}, f32[368]{0:T(512)S(1)}, u32[]{:S(2)}) copy-start(f32[368]{0:T(512)S(1)} %fusion.61) | copy-start | bytes 4420
  11.6 95.8 %copy-start.30 = (f32[1152]{0:T(1024)}, f32[1152]{0:T(1024)S(1)}, u32[]{:S(2)}) copy-start(f32[1152]{0:T(1024)S(1)} %get-tuple-element.75) | copy-start | bytes 13828
  15.0 86.0 %all-gather.11.cloned.1.call-start = ((), (), s32[]{:S(2)}) async-start(), calls=%async_computation.9 | async-start | bytes 4700160 | tf_op jit(solution)/shard_map/all_gather | solution.py:181
  15.9 125.8 %all-gather.13.cloned.1.call-start = ((), (), s32[]{:S(2)}) async-start(), calls=%async_computation.10 | async-start | bytes 1566720 | tf_op jit(solution)/shard_map/all_gather | solution.py:185
  16.6 155.8 %reduce-scatter.17.cloned.1.call-start = ((), (), s32[]{:S(2)}) async-start(), calls=%async_computation.11 | async-start | bytes 2543616 | tf_op jit(solution)/shard_map/reduce_scatter | solution.py:33
  146.0 84.2 %all-gather.17.cloned.1.call-start = ((), (), s32[]{:S(2)}) async-start(), calls=%async_computation.13 | async-start | bytes 5326848 | tf_op jit(solution)/shard_map/all_gather | solution.py:182
  146.8 112.6 %all-gather.15.cloned.1.call-start = ((), (), s32[]{:S(2)}) async-start(), calls=%async_computation.12 | async-start | bytes 2543616 | tf_op jit(solution)/shard_map/all_gather | solution.py:29
  177.2 112.5 %all-gather.21.cloned.1.call-start = ((), (), s32[]{:S(2)}) async-start(), calls=%async_computation.16 | async-start | bytes 2543616 | tf_op jit(solution)/shard_map/all_gather | solution.py:29
  177.9 169.6 %all-gather.19.cloned.1.call-start = ((), (), s32[]{:S(2)}) async-start(), calls=%async_computation.14 | async-start | bytes 5326848 | tf_op jit(solution)/shard_map/all_gather | solution.py:186
  178.7 168.8 %copy-start.46 = (f32[2152]{0:T(1024)S(1)}, f32[2152]{0:T(1024)}, u32[]{:S(2)}) copy-start(f32[2152]{0:T(1024)} %param.51) | copy-start | bytes 25828
  178.8 216.0 %reduce-scatter.21.cloned.1.call-start = ((), (), s32[]{:S(2)}) async-start(), calls=%async_computation.17 | async-start | bytes 2543616 | tf_op jit(solution)/shard_map/reduce_scatter | solution.py:33
  368.7 55.7 %reduce-scatter.19.cloned.1.call-start = ((), (), s32[]{:S(2)}) async-start(), calls=%async_computation.15 | async-start | bytes 2543616 | tf_op jit(solution)/shard_map/reduce_scatter | solution.py:33
  380.0 77.7 %all-gather.23.cloned.1.call-start = ((), (), s32[]{:S(2)}) async-start(), calls=%async_computation.18 | async-start | bytes 2543616 | tf_op jit(solution)/shard_map/all_gather | solution.py:29
  428.9 204.0 %reduce-scatter.29.cloned.1.call-start = ((), (), s32[]{:S(2)}) async-start(), calls=%async_computation.22 | async-start | bytes 1566720
  462.2 172.3 %reduce-scatter.31.cloned.1.call-start = ((), (), s32[]{:S(2)}) async-start(), calls=%async_computation.23 | async-start | bytes 5326848
  472.5 211.1 %reduce-scatter.27.cloned.1.call-start = ((), (), s32[]{:S(2)}) async-start(), calls=%async_computation.21 | async-start | bytes 5326848
  481.7 230.4 %reduce-scatter.23.cloned.1.call-start = ((), (), s32[]{:S(2)}) async-start(), calls=%async_computation.19 | async-start | bytes 2543616 | tf_op jit(solution)/shard_map/reduce_scatter | solution.py:33
  528.6 259.9 %reduce-scatter.25.cloned.1.call-start = ((), (), s32[]{:S(2)}) async-start(), calls=%async_computation.20 | async-start | bytes 4386816
  565.8 146.3 %copy-start.31 = (f32[1152]{0:T(1024)S(1)}, f32[1152]{0:T(1024)}, u32[]{:S(2)}) copy-start(f32[1152]{0:T(1024)} %copy-done.30) | copy-start | bytes 13828
  565.9 146.3 %copy-start.36 = (f32[368]{0:T(512)S(1)}, f32[368]{0:T(512)}, u32[]{:S(2)}) copy-start(f32[368]{0:T(512)} %copy-done.35) | copy-start | bytes 4420
  567.9 146.0 %copy-start.45 = (f32[368]{0:T(512)S(1)}, f32[368]{0:T(512)}, u32[]{:S(2)}) copy-start(f32[368]{0:T(512)} %copy-done.44) | copy-start | bytes 4420
  568.0 146.0 %copy-start.39 = (f32[368]{0:T(512)S(1)}, f32[368]{0:T(512)}, u32[]{:S(2)}) copy-start(f32[368]{0:T(512)} %copy-done.38) | copy-start | bytes 4420
  568.0 148.0 %copy-start.10 = (bf16[1,368,1152]{2,1,0:T(8,128)(2,1)S(1)}, bf16[1,368,1152]{2,1,0:T(8,128)(2,1)}, u32[]{:S(2)}) copy-start(bf16[1,368,1152]{2,1,0:T(8,128)(2,1)} %param.28) | copy-start | bytes 2543620
  716.0 117.2 %copy-start.41 = (f32[2,576]{1,0:T(2,128)S(1)}, f32[2,576]{1,0:T(2,128)}, u32[]{:S(2)}) copy-start(f32[2,576]{1,0:T(2,128)} %param.48) | copy-start | bytes 13828
  716.0 118.5 %copy-start.37 = (f32[2,1152]{1,0:T(2,128)S(1)}, f32[2,1152]{1,0:T(2,128)}, u32[]{:S(2)}) copy-start(f32[2,1152]{1,0:T(2,128)} %param.42) | copy-start | bytes 27652
  716.0 121.2 %copy-start.34 = (f32[4,1152]{1,0:T(4,128)S(1)}, f32[4,1152]{1,0:T(4,128)}, u32[]{:S(2)}) copy-start(f32[4,1152]{1,0:T(4,128)} %param.45) | copy-start | bytes 55300
  716.1 121.2 %copy-start.42 = (f32[4,1152]{1,0:T(4,128)S(1)}, f32[4,1152]{1,0:T(4,128)}, u32[]{:S(2)}) copy-start(f32[4,1152]{1,0:T(4,128)} %param.46) | copy-start | bytes 55300
  716.1 121.2 %copy-start.43 = (f32[4,1152]{1,0:T(4,128)S(1)}, f32[4,1152]{1,0:T(4,128)}, u32[]{:S(2)}) copy-start(f32[4,1152]{1,0:T(4,128)} %param.47) | copy-start | bytes 55300
  759.4 81.7 %copy-start.32 = (f32[576,72]{0,1:T(8,128)S(1)}, f32[576,72]{0,1:T(8,128)}, u32[]{:S(2)}) copy-start(f32[576,72]{0,1:T(8,128)} %param.34) | copy-start | bytes 497668
  759.4 81.7 %copy-start.33 = (f32[576,72]{0,1:T(8,128)S(1)}, f32[576,72]{0,1:T(8,128)}, u32[]{:S(2)}) copy-start(f32[576,72]{0,1:T(8,128)} %param.35) | copy-start | bytes 497668
  (34 other events, 381.3 us)
Sparse Core Ops, SparseCore 0:
  15.2 31.2 all-gather.8
  49.3 51.7 all-gather.10
  103.8 37.8 all-gather.12
  146.1 26.2 reduce-scatter.16
  175.2 54.8 all-gather.16
  232.2 27.1 all-gather.14
  261.0 28.5 all-gather.20
  292.6 54.9 all-gather.18
  368.8 25.9 reduce-scatter.20
  396.9 27.4 reduce-scatter.18
  429.1 28.5 all-gather.22
  462.3 58.7 reduce-scatter.28
  525.6 77.2 reduce-scatter.30
  606.7 76.8 reduce-scatter.26
  685.8 26.2 reduce-scatter.22
  715.9 72.6 reduce-scatter.24
where the time goes:
time: 859 us; the launch traced here: 853 us
  waiting for transfers between devices  442 us (51%)
  blocking collectives  142 us (17%)
  matrix products  124 us (14%)
  other arithmetic  79.5 us (9%)
  local copies, waits for them, and re-layouts  40.6 us (5%)
  between operations  22.6 us (3%)
    all_gather x4, waiting for transfers between devices, whole_rows(): return lax.all_gather(part, 'tensor', axis=1, tiled=True)  107 us
    reduce_scatter x4, waiting for transfers between devices, share_rows(): lax.psum_scatter(full.astype(jnp.bfloat16), 'tensor', scatter_dimension=1...  94.5 us
    unnamed x20, waiting for transfers between devices  75.5 us
    psum x1, blocking collectives, on_device(): head_sum, hidden_sum = lax.psum((head_grad, hidden_grad), 'dp')  62.1 us
    all_gather x1, waiting for transfers between devices, on_device(): lax.all_gather(reduce_weight.astype(jnp.bfloat16), 'dp', axis=1, tiled=True)  57.9 us
    all_gather x1, waiting for transfers between devices, on_device(): lax.all_gather(joint_weight.astype(jnp.bfloat16), 'dp', axis=0, tiled=True)  54.5 us
    all_gather x1, waiting for transfers between devices, on_device(): lax.all_gather(expand_weight.astype(jnp.bfloat16), 'dp', axis=0, tiled=True)  50.8 us
    psum x1, blocking collectives, on_device(): gain_sum, shift_sum = lax.psum((gain_grad, shift_grad), ('dp', 'tensor'))  40.8 us
  transfers between devices with their start and end apart: 16, of which 14 were waited for; matrix products, arithmetic and copies ran while one was open for 22% of the time, Pallas kernels for 0%

commit v1 on v0

--- a/solution.py
+++ b/solution.py
@@ -12,6 +12,18 @@
 decay_rate = 0.1
 adam_eps = 1e-08
 mask_fill = -1e30
+
+
+def doubled_up(x, axis, dim):
+    ways, here = (lax.axis_size(axis), lax.axis_index(axis))
+    grown, reach = (x, 1)
+    while reach < ways:
+        theirs = lax.ppermute(grown, axis, [(d, d ^ reach) for d in range(ways)])
+        mine_first = jnp.concatenate([grown, theirs], axis=dim)
+        theirs_first = jnp.concatenate([theirs, grown], axis=dim)
+        grown = jnp.where(here & reach == 0, mine_first, theirs_first)
+        reach = 2 * reach
+    return grown
 
 
 def layer_norm(values, gain, shift):
@@ -179,7 +191,7 @@
 ):
     first_pair = (
         lax.all_gather(joint_weight.astype(jnp.bfloat16), "dp", axis=0, tiled=True),
-        lax.all_gather(expand_weight.astype(jnp.bfloat16), "dp", axis=0, tiled=True),
+        doubled_up(expand_weight.astype(jnp.bfloat16), "dp", 0),
     )
     second_pair = (
         lax.all_gather(output_weight.astype(jnp.bfloat16), "dp", axis=1, tiled=True),

time: 859 us -> 898 us (1.045)
  waiting for transfers between devices: 442 us -> 467 us
    ppermute x0 -> x4, waiting for transfers between devices: none -> 181 us  [doubled_up(): theirs = lax.ppermute(grown, axis, [(d, d ^ reach) for d in range(ways)])]
    all_gather x1, waiting for transfers between devices: 57.9 us -> 0.01 us  [on_device(): lax.all_gather(reduce_weight.astype(jnp.bfloat16), 'dp', axis=1, tiled=True)]
    all_gather x1 -> x0, waiting for transfers between devices: 50.8 us -> none  [on_device(): lax.all_gather(expand_weight.astype(jnp.bfloat16), 'dp', axis=0, tiled=True)]
    all_gather x4, waiting for transfers between devices: 107 us -> 57.7 us  [whole_rows(): return lax.all_gather(part, 'tensor', axis=1, tiled=True)]
    unnamed x20 -> x19, waiting for transfers between devices: 75.5 us -> 75.3 us
    unnamed x103 -> x105, local copies, waits for them, and re-layouts: 38.6 us -> 38.6 us
  transfers between devices with their start and end apart: 16 -> 19, of which waited for: 14 -> 14; matrix products, arithmetic and copies ran while one was open for 22% -> 21% of each run, Pallas kernels for 0% -> 0%
where the time goes in v1:
time: 898 us; the launch traced here: 893 us
  waiting for transfers between devices  467 us (52%)
  blocking collectives  142 us (16%)
  matrix products  128 us (14%)
  other arithmetic  84.8 us (9%)
  local copies, waits for them, and re-layouts  40.6 us (5%)
  between operations  22.7 us (3%)
    ppermute x4, waiting for transfers between devices, doubled_up(): theirs = lax.ppermute(grown, axis, [(d, d ^ reach) for d in range(ways)])  181 us
    reduce_scatter x4, waiting for transfers between devices, share_rows(): lax.psum_scatter(full.astype(jnp.bfloat16), 'tensor', scatter_dimension=1...  97.1 us
    unnamed x19, waiting for transfers between devices  75.3 us
    psum x1, blocking collectives, on_device(): head_sum, hidden_sum = lax.psum((head_grad, hidden_grad), 'dp')  62.1 us
    all_gather x4, waiting for transfers between devices, whole_rows(): return lax.all_gather(part, 'tensor', axis=1, tiled=True)  57.7 us
    all_gather x1, waiting for transfers between devices, on_device(): lax.all_gather(joint_weight.astype(jnp.bfloat16), 'dp', axis=0, tiled=True)  54.5 us
    psum x1, blocking collectives, on_device(): gain_sum, shift_sum = lax.psum((gain_grad, shift_grad), ('dp', 'tensor'))  40.8 us
    psum x1, blocking collectives, on_device(): lax.psum(owned + shared + everywhere, ('dp', 'tensor'))  39.4 us
  transfers between devices with their start and end apart: 19, of which 14 were waited for; matrix products, arithmetic and copies ran while one was open for 21% of the time, Pallas kernels for 0%

profile of v1, /device:TPU:0, one launch (start us, length us, event | category | flops | bytes accessed | tf_op | source)
XLA Modules:
  0.0 892.5 jit_solution(4949663519779372942)
XLA Ops:
  17.5 29.0 %all-gather.8.cloned.1.call-done = bf16[1,736,1152]{2,1,0:T(8,128)(2,1)} async-done(((bf16[1,368,1152]{2,1,0:T(8,128)(2,1)}), bf16[1,736,1152]{2,1,0:T(8,128)(2,1)}) %all-gather.8.cloned.1.call-update) | async-done | bytes 1695760 | tf_op jit(solution)/shard_map/all_gather | solution.py:41
  46.5 54.5 %all-gather.10.cloned.1.call-done = bf16[1152,3,576]{2,0,1:T(8,128)(2,1)} async-done(((bf16[72,3,576]{2,0,1:T(8,128)(2,1)}), bf16[1152,3,576]{2,0,1:T(8,128)(2,1)}) %all-gather.10.cloned.1.call-update) | async-done | bytes 3981328 | tf_op jit(solution)/shard_map/all_gather | solution.py:193
  101.0 6.4 add_convert_fusion
  107.7 8.8 fusion
  116.5 10.0 %exponential_reduce_fusion = f32[8,736]{1,0:T(8,128)S(1)} fusion(f32[8,736,736]{1,2,0:T(8,128)} %get-tuple-element.122, f32[8,736]{1,0:T(8,128)S(1)} %get-tuple-element.121, pred[736]{0:T(1024)(128)(4,1)S(1)} %iota_compare_fusion), kind=kLoop, calls=%fused_computation.3 | loop fusion | flops 17328384 | bytes 17382112 | tf_op jit(solution)/shard_map/while/body/eval_jaxpr/reduce_sum | solution.py:78
  126.6 8.2 fusion.1
  146.0 26.4 %reduce-scatter.17.cloned.1.call-done = bf16[1,368,1152]{2,1,0:T(8,128)(2,1)} async-done(((bf16[1,736,1152]{2,1,0:T(8,128)(2,1)}), bf16[1,368,1152]{2,1,0:T(8,128)(2,1)}) %reduce-scatter.17.cloned.1.call-update) | async-done | bytes 847888 | tf_op jit(solution)/shard_map/reduce_scatter | solution.py:45
  182.2 14.8 %collective-permute-done.1 = bf16[144,2152]{1,0:T(8,128)(2,1)} collective-permute-done((bf16[144,2152]{1,0:T(8,128)(2,1)S(1)}, bf16[144,2152]{1,0:T(8,128)(2,1)}, u32[]{:S(2)}, u32[]{:S(2)}) %collective-permute-start.1) | collective-permute-done | bytes 619808 | tf_op jit(solution)/shard_map/ppermute | solution.py:21
  200.6 27.4 %collective-permute-done.2 = bf16[288,2152]{1,0:T(8,128)(2,1)} collective-permute-done((bf16[288,2152]{1,0:T(8,128)(2,1)S(1)}, bf16[288,2152]{1,0:T(8,128)(2,1)}, u32[]{:S(2)}, u32[]{:S(2)}) %collective-permute-start.2) | collective-permute-done | bytes 1239584 | tf_op jit(solution)/shard_map/ppermute | solution.py:21
  234.3 137.4 %collective-permute-done.3 = bf16[576,2152]{1,0:T(8,128)(2,1)} collective-permute-done((bf16[576,2152]{1,0:T(8,128)(2,1)}, bf16[576,2152]{1,0:T(8,128)(2,1)}, u32[]{:S(2)}, u32[]{:S(2)}) %collective-permute-start.3) | collective-permute-done | bytes 2479136 | tf_op jit(solution)/shard_map/ppermute | solution.py:21
  371.7 11.6 %fusion.38 = f32[736,2152]{1,0:T(8,128)} fusion(bf16[1,736,1152]{2,1,0:T(8,128)(2,1)} %all-gather.14.cloned.1.call-done, bf16[576,2152]{1,0:T(8,128)(2,1)} %collective-permute-done.3, bf16[576,2152]{1,0:T(8,128)(2,1)} %maximum_select_fusion.1, pred[]{:T(512)S(6)} %eq.12), kind=kOutput, calls=%fused_computation.74 | convolution fusion | flops 3671553024 | bytes 12989441 | tf_op jit(solution)/shard_map/bsd,df->bsf/dot_general | solution.py:127
  383.3 11.3 %convert_reduce_fusion = (f32[2152]{0:T(1024)S(1)}, bf16[736,2152]{1,0:T(8,128)(2,1)S(1)}) fusion(f32[736,2152]{1,0:T(8,128)} %fusion.38, f32[2152]{0:T(1024)S(1)} %copy-done.47, bf16[2152,1152]{0,1:T(8,128)(2,1)} %all-gather.16.cloned.1.call-done, bf16[1,736,1152]{2,1,0:T(8,128)(2,1)} %all-gather.18.cloned.1.call-done), kind=kOutput, calls=%fused_computation.18 | convolution fusion | flops 3685668096 | bytes 16174400 | tf_op jit(solution)/shard_map/bsd,fd->bsf/dot_general | solution.py:211
  396.2 9.7 %fusion.13 = bf16[1,736,1152]{2,1,0:T(8,128)(2,1)} fusion(bf16[736,2152]{1,0:T(8,128)(2,1)S(1)} %get-tuple-element.126, bf16[576,2152]{1,0:T(8,128)(2,1)} %collective-permute-done.3, bf16[576,2152]{1,0:T(8,128)(2,1)} %maximum_select_fusion.1, pred[]{:T(512)S(6)} %eq.12), kind=kOutput, calls=%fused_computation.33 | convolution fusion | flops 3672400896 | bytes 9821697 | tf_op jit(solution)/shard_map/bsf,df->bsd/dot_general | solution.py:220
  406.2 11.1 %fusion.12 = bf16[1,736,1152]{2,1,0:T(8,128)(2,1)} fusion(bf16[2152,1152]{0,1:T(8,128)(2,1)} %all-gather.16.cloned.1.call-done, f32[736,2152]{1,0:T(8,128)} %fusion.38, f32[2152]{0:T(1024)S(1)} %copy-done.47), kind=kOutput, calls=%fused_computation.32 | convolution fusion | flops 3665927680 | bytes 12998048 | tf_op jit(solution)/shard_map/bsf,fd->bsd/dot_general | solution.py:133
  417.4 16.2 %reduce-scatter.21.cloned.1.call-done = bf16[1,368,1152]{2,1,0:T(8,128)(2,1)} async-done(((bf16[1,736,1152]{2,1,0:T(8,128)(2,1)}), bf16[1,368,1152]{2,1,0:T(8,128)(2,1)}) %reduce-scatter.21.cloned.1.call-update) | async-done | bytes 847888 | tf_op jit(solution)/shard_map/reduce_scatter | solution.py:45
  435.6 27.7 %reduce-scatter.19.cloned.1.call-done = bf16[1,368,1152]{2,1,0:T(8,128)(2,1)} async-done(((bf16[1,736,1152]{2,1,0:T(8,128)(2,1)}), bf16[1,368,1152]{2,1,0:T(8,128)(2,1)}) %reduce-scatter.19.cloned.1.call-update) | async-done | bytes 847888 | tf_op jit(solution)/shard_map/reduce_scatter | solution.py:45
  467.9 28.7 %all-gather.20.cloned.1.call-done = bf16[1,736,1152]{2,1,0:T(8,128)(2,1)} async-done(((bf16[1,368,1152]{2,1,0:T(8,128)(2,1)}), bf16[1,736,1152]{2,1,0:T(8,128)(2,1)}) %all-gather.20.cloned.1.call-update) | async-done | bytes 1695760 | tf_op jit(solution)/shard_map/all_gather | solution.py:41
  501.5 10.1 %convolution_convert_fusion = bf16[2152,1152]{0,1:T(8,128)(2,1)} fusion(bf16[1,736,1152]{2,1,0:T(8,128)(2,1)} %all-gather.18.cloned.1.call-done, f32[736,2152]{1,0:T(8,128)} %fusion.38, f32[2152]{0:T(1024)S(1)} %copy-done.47), kind=kOutput, calls=%fused_computation.6 | convolution fusion | flops 3667558912 | bytes 12998048 | tf_op jit(solution)/shard_map/bsf,bsd->fd/dot_general | solution.py:210
  511.7 9.1 %convolution_convert_fusion.1 = bf16[1152,2152]{1,0:T(8,128)(2,1)} fusion(bf16[736,2152]{1,0:T(8,128)(2,1)} %copy-done.48, bf16[1,736,1152]{2,1,0:T(8,128)(2,1)} %all-gather.14.cloned.1.call-done), kind=kOutput, calls=%fused_computation.7 | convolution fusion | flops 3651720192 | bytes 9821696 | tf_op jit(solution)/shard_map/bsd,bsf->df/dot_general | solution.py:215
  524.1 6.4 convolution_convert_fusion.7
  530.5 13.1 %multiply_reduce_fusion = (f32[8,736]{1,0:T(8,128)S(1)}, f32[8,736,736]{1,2,0:T(8,128)}) fusion(f32[8,736,736]{1,2,0:T(8,128)} %get-tuple-element.122, f32[8,736]{1,0:T(8,128)S(1)} %log_add_fusion, pred[736]{0:T(1024)(128)(4,1)S(1)} %iota_compare_fusion, bf16[736,8,72]{0,2,1:T(8,128)(2,1)S(1)} %bitcast.106, bf16[736,8,72]{0,2,1:T(8,128)(2,1)S(1)} %bitcast.91), kind=kOutput, calls=%fused_computation.1 | convolution fusion | flops 645695744 | bytes 36412128 | tf_op jit(solution)/shard_map/while/body/eval_jaxpr/qhd,khd->hqk/dot_general | solution.py:96
  543.6 13.0 %multiply_convert_fusion = bf16[8,736,736]{1,2,0:T(8,128)(2,1)S(1)} fusion(f32[8,736,736]{1,2,0:T(8,128)} %get-tuple-element.124, f32[8,736,736]{1,2,0:T(8,128)} %get-tuple-element.122, f32[8,736]{1,0:T(8,128)S(1)} %get-tuple-element.123, f32[8,736]{1,0:T(8,128)S(1)} %log_add_fusion, pred[736]{0:T(1024)(128)(4,1)S(1)} %iota_compare_fusion), kind=kLoop, calls=%fused_computation | loop fusion | flops 26001408 | bytes 43383520 | tf_op jit(solution)/shard_map/while/body/eval_jaxpr/convert_element_type | solution.py:98
  562.1 5.5 fusion.11
  567.9 6.3 convolution_convert_fusion.2
  574.2 18.2 %copy.70 = bf16[1152,3,576]{2,1,0:T(4,128)(2,1)} copy(bf16[1152,3,576]{2,0,1:T(8,128)(2,1)S(1)} %convolution_convert_fusion.2) | data formatting | bytes 7962624
  592.4 12.3 %reshape.392 = bf16[1152,1728]{1,0:T(8,128)(2,1)} reshape(bf16[1152,3,576]{2,1,0:T(4,128)(2,1)} %copy.70) | data formatting | bytes 7962624
  607.3 62.1 %all-reduce.4 = (f32[2,576]{1,0:T(2,128)S(1)}, f32[2152]{0:T(1024)S(1)}) all-reduce(f32[2,576]{1,0:T(2,128)S(1)} %convert_reduce_fusion.1, f32[2152]{0:T(1024)S(1)} %get-tuple-element.125), channel_id=1, replica_groups=mesh['dp'=16,'tensor'=2] {'dp'}, use_global_device_ids=true, to_apply=%region_24.25 | all-reduce | flops 3304 | bytes 26432 | tf_op jit(solution)/shard_map/psum | solution.py:255
  675.2 47.3 %reduce-scatter.27.cloned.1.call-done = bf16[72,2152]{1,0:T(8,128)(2,1)} async-done(((bf16[1152,2152]{1,0:T(8,128)(2,1)}), bf16[72,2152]{1,0:T(8,128)(2,1)}) %reduce-scatter.27.cloned.1.call-update) | async-done | bytes 309904
  724.2 26.9 %reduce-scatter.23.cloned.1.call-done = bf16[1,368,1152]{2,1,0:T(8,128)(2,1)} async-done(((bf16[1,736,1152]{2,1,0:T(8,128)(2,1)}), bf16[1,368,1152]{2,1,0:T(8,128)(2,1)}) %reduce-scatter.23.cloned.1.call-update) | async-done | bytes 847888 | tf_op jit(solution)/shard_map/reduce_scatter | solution.py:45
  756.9 40.8 %all-reduce.3 = (f32[2,1152]{1,0:T(2,128)S(1)}, f32[4,1152]{1,0:T(4,128)S(1)}) all-reduce(f32[2,1152]{1,0:T(2,128)S(1)} %pad_maximum_fusion.6, f32[4,1152]{1,0:T(4,128)S(1)} %pad_maximum_fusion.4), channel_id=1, replica_groups=mesh['dp'=16,'tensor'=2] {'dp','tensor'}, use_global_device_ids=true, to_apply=%region_31.32 | all-reduce | flops 6912 | bytes 55296 | tf_op jit(solution)/shard_map/psum | solution.py:254
  800.3 27.3 %reduce-scatter.25.cloned.1.call-done = bf16[72,1728]{1,0:T(8,128)(2,1)} async-done(((bf16[1152,1728]{1,0:T(8,128)(2,1)}), bf16[72,1728]{1,0:T(8,128)(2,1)}) %reduce-scatter.25.cloned.1.call-update) | async-done | bytes 248848
  832.0 39.4 %psum.39 = f32[]{:T(128)} all-reduce(f32[]{:T(128)S(6)} %add.313), channel_id=1, replica_groups=mesh['dp'=16,'tensor'=2] {'dp','tensor'}, use_global_device_ids=true, to_apply=%region_39.40 | all-reduce | flops 1 | bytes 8 | tf_op jit(solution)/shard_map/psum | solution.py:261
  (212 shorter events, 92.9 us)
Async XLA Ops:
  7.2 39.3 %all-gather.8.cloned.1.call-start = ((), (), s32[]{:S(2)}) async-start(), calls=%async_computation.8 | async-start | bytes 2543616 | tf_op jit(solution)/shard_map/all_gather | solution.py:41
  8.7 98.8 %copy-start.36 = (f32[368]{0:T(512)}, f32[368]{0:T(512)S(1)}, u32[]{:S(2)}) copy-start(f32[368]{0:T(512)S(1)} %broadcast_multiply_fusion.1) | copy-start | bytes 4420
  10.8 96.6 %copy-start.39 = (f32[368]{0:T(512)}, f32[368]{0:T(512)S(1)}, u32[]{:S(2)}) copy-start(f32[368]{0:T(512)S(1)} %fusion.61) | copy-start | bytes 4420
  15.0 86.0 %all-gather.10.cloned.1.call-start = ((), (), s32[]{:S(2)}) async-start(), calls=%async_computation.9 | async-start | bytes 4700160 | tf_op jit(solution)/shard_map/all_gather | solution.py:193
  15.9 125.8 %all-gather.12.cloned.1.call-start = ((), (), s32[]{:S(2)}) async-start(), calls=%async_computation.10 | async-start | bytes 1566720 | tf_op jit(solution)/shard_map/all_gather | solution.py:197
  16.6 155.8 %reduce-scatter.17.cloned.1.call-start = ((), (), s32[]{:S(2)}) async-start(), calls=%async_computation.11 | async-start | bytes 2543616 | tf_op jit(solution)/shard_map/reduce_scatter | solution.py:45
  146.0 225.7 %all-gather.14.cloned.1.call-start = ((), (), s32[]{:S(2)}) async-start(), calls=%async_computation.12 | async-start | bytes 2543616 | tf_op jit(solution)/shard_map/all_gather | solution.py:41
  177.2 206.1 %all-gather.18.cloned.1.call-start = ((), (), s32[]{:S(2)}) async-start(), calls=%async_computation.15 | async-start | bytes 2543616 | tf_op jit(solution)/shard_map/all_gather | solution.py:41
  177.8 205.5 %all-gather.16.cloned.1.call-start = ((), (), s32[]{:S(2)}) async-start(), calls=%async_computation.13 | async-start | bytes 5326848 | tf_op jit(solution)/shard_map/all_gather | solution.py:198
  178.6 254.9 %reduce-scatter.21.cloned.1.call-start = ((), (), s32[]{:S(2)}) async-start(), calls=%async_computation.16 | async-start | bytes 2543616 | tf_op jit(solution)/shard_map/reduce_scatter | solution.py:45
  178.9 1.7 collective-permute-start
  180.7 16.3 %collective-permute-start.1 = (bf16[144,2152]{1,0:T(8,128)(2,1)S(1)}, bf16[144,2152]{1,0:T(8,128)(2,1)}, u32[]{:S(2)}, u32[]{:S(2)}) collective-permute-start(bf16[144,2152]{1,0:T(8,128)(2,1)S(1)} %maximum_select_fusion.5), channel_id=1, source_target_pairs={{0,4},{2,6},{4,0},{6,2},{8,12},{10,14},{12,8},{14,10},{16,20},{18,... | collective-permute-start | bytes 1859336 | tf_op jit(solution)/shard_map/ppermute | solution.py:21
  199.1 28.9 %collective-permute-start.2 = (bf16[288,2152]{1,0:T(8,128)(2,1)S(1)}, bf16[288,2152]{1,0:T(8,128)(2,1)}, u32[]{:S(2)}, u32[]{:S(2)}) collective-permute-start(bf16[288,2152]{1,0:T(8,128)(2,1)S(1)} %maximum_select_fusion.2), channel_id=1, source_target_pairs={{0,8},{2,10},{4,12},{6,14},{8,0},{10,2},{12,4},{14,6},{16,24},{18,... | collective-permute-start | bytes 3718664 | tf_op jit(solution)/shard_map/ppermute | solution.py:21
  231.9 139.9 %collective-permute-start.3 = (bf16[576,2152]{1,0:T(8,128)(2,1)}, bf16[576,2152]{1,0:T(8,128)(2,1)}, u32[]{:S(2)}, u32[]{:S(2)}) collective-permute-start(bf16[576,2152]{1,0:T(8,128)(2,1)} %maximum_select_fusion.1), channel_id=1, source_target_pairs={{0,16},{2,18},{4,20},{6,22},{8,24},{10,26},{12,28},{14,30},{16,0},... | collective-permute-start | bytes 7437320 | tf_op jit(solution)/shard_map/ppermute | solution.py:21
  234.3 149.0 %copy-start.47 = (f32[2152]{0:T(1024)S(1)}, f32[2152]{0:T(1024)}, u32[]{:S(2)}) copy-start(f32[2152]{0:T(1024)} %param.51) | copy-start | bytes 25828
  405.9 57.3 %reduce-scatter.19.cloned.1.call-start = ((), (), s32[]{:S(2)}) async-start(), calls=%async_computation.14 | async-start | bytes 2543616 | tf_op jit(solution)/shard_map/reduce_scatter | solution.py:45
  417.3 79.3 %all-gather.20.cloned.1.call-start = ((), (), s32[]{:S(2)}) async-start(), calls=%async_computation.17 | async-start | bytes 2543616 | tf_op jit(solution)/shard_map/all_gather | solution.py:41
  467.8 204.0 %reduce-scatter.29.cloned.1.call-start = ((), (), s32[]{:S(2)}) async-start(), calls=%async_computation.21 | async-start | bytes 1566720
  501.1 172.3 %reduce-scatter.31.cloned.1.call-start = ((), (), s32[]{:S(2)}) async-start(), calls=%async_computation.22 | async-start | bytes 5326848
  511.6 210.9 %reduce-scatter.27.cloned.1.call-start = ((), (), s32[]{:S(2)}) async-start(), calls=%async_computation.20 | async-start | bytes 5326848
  520.8 230.3 %reduce-scatter.23.cloned.1.call-start = ((), (), s32[]{:S(2)}) async-start(), calls=%async_computation.18 | async-start | bytes 2543616 | tf_op jit(solution)/shard_map/reduce_scatter | solution.py:45
  567.6 259.9 %reduce-scatter.25.cloned.1.call-start = ((), (), s32[]{:S(2)}) async-start(), calls=%async_computation.19 | async-start | bytes 4386816
  604.8 146.2 %copy-start.32 = (f32[1152]{0:T(1024)S(1)}, f32[1152]{0:T(1024)}, u32[]{:S(2)}) copy-start(f32[1152]{0:T(1024)} %copy-done.31) | copy-start | bytes 13828
  604.8 146.2 %copy-start.37 = (f32[368]{0:T(512)S(1)}, f32[368]{0:T(512)}, u32[]{:S(2)}) copy-start(f32[368]{0:T(512)} %copy-done.36) | copy-start | bytes 4420
  606.9 146.0 %copy-start.46 = (f32[368]{0:T(512)S(1)}, f32[368]{0:T(512)}, u32[]{:S(2)}) copy-start(f32[368]{0:T(512)} %copy-done.45) | copy-start | bytes 4420
  606.9 146.0 %copy-start.40 = (f32[368]{0:T(512)S(1)}, f32[368]{0:T(512)}, u32[]{:S(2)}) copy-start(f32[368]{0:T(512)} %copy-done.39) | copy-start | bytes 4420
  606.9 148.0 %copy-start.10 = (bf16[1,368,1152]{2,1,0:T(8,128)(2,1)S(1)}, bf16[1,368,1152]{2,1,0:T(8,128)(2,1)}, u32[]{:S(2)}) copy-start(bf16[1,368,1152]{2,1,0:T(8,128)(2,1)} %param.28) | copy-start | bytes 2543620
  755.0 117.2 %copy-start.42 = (f32[2,576]{1,0:T(2,128)S(1)}, f32[2,576]{1,0:T(2,128)}, u32[]{:S(2)}) copy-start(f32[2,576]{1,0:T(2,128)} %param.48) | copy-start | bytes 13828
  755.0 118.5 %copy-start.38 = (f32[2,1152]{1,0:T(2,128)S(1)}, f32[2,1152]{1,0:T(2,128)}, u32[]{:S(2)}) copy-start(f32[2,1152]{1,0:T(2,128)} %param.42) | copy-start | bytes 27652
  755.0 121.2 %copy-start.35 = (f32[4,1152]{1,0:T(4,128)S(1)}, f32[4,1152]{1,0:T(4,128)}, u32[]{:S(2)}) copy-start(f32[4,1152]{1,0:T(4,128)} %param.45) | copy-start | bytes 55300
  755.0 121.2 %copy-start.43 = (f32[4,1152]{1,0:T(4,128)S(1)}, f32[4,1152]{1,0:T(4,128)}, u32[]{:S(2)}) copy-start(f32[4,1152]{1,0:T(4,128)} %param.46) | copy-start | bytes 55300
  755.0 121.2 %copy-start.44 = (f32[4,1152]{1,0:T(4,128)S(1)}, f32[4,1152]{1,0:T(4,128)}, u32[]{:S(2)}) copy-start(f32[4,1152]{1,0:T(4,128)} %param.47) | copy-start | bytes 55300
  (38 other events, 645.3 us)
Sparse Core Ops, SparseCore 0:
  15.2 31.2 all-gather.7
  49.3 51.7 all-gather.9
  103.8 37.8 all-gather.11
  146.1 26.2 reduce-scatter.16
  177.3 28.5 all-gather.13
  207.4 28.5 all-gather.17
  239.0 104.6 all-gather.15
  406.0 27.4 reduce-scatter.20
  435.8 27.4 reduce-scatter.18
  468.0 28.5 all-gather.19
  501.2 58.7 reduce-scatter.28
  564.4 77.2 reduce-scatter.30
  645.6 76.7 reduce-scatter.26
  724.7 26.3 reduce-scatter.22
  754.8 72.6 reduce-scatter.24
